TPU v7x, 256 devices: a whole 4x4x8 slice. The times are simulated.
256 devices in a mesh: lat: 2 (over x_hi), dp: 64 (over z, y, core), exp: 2 (over x_lo).
Axes of the slice: x: 4 (x_hi: 2, x_lo: 2; x = x_hi * 2 + x_lo), y: 4, z: 8, core: 2. Of those that a mesh axis runs over, the one named last changes fastest.
Arguments:
- images: bfloat16 [128, 32, 256, 192], P(('dp', 'exp'), 'lat'), may hold values from -6 to 6
- cotangent: bfloat16 [128, 32, 256, 192], P(('dp', 'exp'), 'lat'), may hold values from -0.0625 to 0.0625
- labels: int32 [128, 32, 2, 1], P(('dp', 'exp'), 'lat'), may hold values from 0 to 15; in each aligned block of 32 rows (0 to 31, 32 to 63, ..., all dimensions but the last counted through in order) at most 3 rows name the same one
- dw_kernel: float32 [7, 7, 192], replicated, may hold values from -0.875 to 0.875
- ln_gain: float32 [192], replicated, may hold values from 0.5 to 2
- w_expand: bfloat16 [192, 768], replicated, may hold values from -0.4375 to 0.4375
- w_reduce: bfloat16 [768, 192], replicated, may hold values from -0.21875 to 0.21875
- exp_in: bfloat16 [16, 192, 768], P('exp'), may hold values from -0.4375 to 0.4375
- exp_out: bfloat16 [16, 768, 192], P('exp'), may hold values from -0.21875 to 0.21875
Outputs:
- output: bfloat16 [128, 32, 256, 192], P(('dp', 'exp'), 'lat')
- grad_in: float32 [16, 192, 768], P('exp')
- grad_out: float32 [16, 768, 192], P('exp')
Inputs may be any that keep to these rules, and one draw needn't show every extreme that they name: `labels`: among the 32 row blocks of one device (aligned runs of 32 blocks in the order clip, row, block), no class is named more than 3 times, a bound that some block reaches.
All inputs are finite; a program needn't handle non-finite values.
Results may differ from a plain program's by a relative error of at most 0.0072.
Values may be sent and summed in bfloat16 or wider, within the bound.
A program may use at most 128 MiB of HBM per device.

v0:
```python
import jax
import jax.numpy as jnp
from jax import lax
from jax.sharding import PartitionSpec as P

EXPERTS = 16
BLOCK = 128
CAP = 3


def with_halo(block, sides, width):
    for axis, dim in sides:
        count = lax.axis_size(axis)
        forward = [(i, i + 1) for i in range(count - 1)]
        backward = [(target, source) for source, target in forward]
        low = lax.ppermute(
            lax.slice_in_dim(block, block.shape[dim] - width, None, axis=dim), axis, forward
        )
        high = lax.ppermute(lax.slice_in_dim(block, 0, width, axis=dim), axis, backward)
        block = jnp.concatenate([low, block, high], axis=dim)
    return block


def gelu_slope(values):
    return (
        0.5 * (1.0 + lax.erf(values * 0.7071067811865476))
        + values * jnp.exp(-0.5 * values * values) * 0.3989422804014327
    )


def depthwise(padded, kernel):
    row_count = padded.shape[1] - 6
    col_count = padded.shape[2] - 6
    summed = jnp.zeros((padded.shape[0], row_count, col_count, padded.shape[3]), jnp.float32)
    for row_off in range(7):
        for col_off in range(7):
            window = padded[:, row_off : row_off + row_count, col_off : col_off + col_count, :]
            summed = summed + window.astype(jnp.float32) * kernel[row_off, col_off]
    return summed


def widen(picture):
    return jnp.pad(picture, ((0, 0), (0, 0), (3, 3), (0, 0)))


def dense_block(images, smoothed, ln_gain, w_expand, w_reduce):
    channels = images.shape[-1]
    channel_mean = jnp.mean(smoothed, axis=-1, keepdims=True)
    centered = smoothed - channel_mean
    variance = jnp.mean(centered * centered, axis=-1, keepdims=True)
    normed = (centered * lax.rsqrt(variance + 1e-06) * ln_gain).astype(jnp.bfloat16)
    flat_normed = normed.reshape(-1, channels)
    expanded = jnp.dot(flat_normed, w_expand, preferred_element_type=jnp.float32)
    active = jax.nn.gelu(expanded, approximate=False).astype(jnp.bfloat16)
    reduced = jnp.dot(active, w_reduce, preferred_element_type=jnp.float32)
    dense_out = images.reshape(-1, channels).astype(jnp.float32) + reduced
    return dense_out.astype(jnp.bfloat16).reshape(images.shape)


def expert_pass(inputs, grads_in, w_in, w_out):
    pre_act = jnp.dot(inputs, w_in, preferred_element_type=jnp.float32)
    hidden = jax.nn.gelu(pre_act, approximate=False).astype(jnp.bfloat16)
    outputs = jnp.dot(hidden, w_out, preferred_element_type=jnp.float32).astype(jnp.bfloat16)
    grad_out = jnp.dot(hidden.T, grads_in, preferred_element_type=jnp.float32)
    back_prop = jnp.dot(grads_in, w_out.T, preferred_element_type=jnp.float32)
    scaled = (back_prop * gelu_slope(pre_act)).astype(jnp.bfloat16)
    grad_in = jnp.dot(inputs.T, scaled, preferred_element_type=jnp.float32)
    return (outputs, grad_in, grad_out)


def body(images, cotangent, labels, dw_kernel, ln_gain, w_expand, w_reduce, exp_in, exp_out):
    channels = images.shape[-1]
    padded = with_halo(images, (("lat", 1),), 3)
    smoothed = depthwise(widen(padded), dw_kernel)
    dense_out = dense_block(images, smoothed, ln_gain, w_expand, w_reduce)
    block_width = BLOCK * channels
    blocks = dense_out.reshape(-1, block_width)
    grad_blocks = cotangent.reshape(-1, block_width)
    flat_labels = labels.reshape(-1)
    members = (flat_labels[:, None] == jnp.arange(EXPERTS, dtype=jnp.int32)[None, :]).astype(
        jnp.int32
    )
    before = jnp.sum(jnp.cumsum(members, axis=0) * members, axis=1) - 1
    slot_of = flat_labels * CAP + before
    placer = (jnp.arange(EXPERTS * CAP, dtype=jnp.int32)[:, None] == slot_of[None, :]).astype(
        jnp.bfloat16
    )
    outgoing = (
        jnp.dot(placer, blocks, preferred_element_type=jnp.float32)
        .astype(jnp.bfloat16)
        .reshape(EXPERTS, CAP, block_width)
    )
    outgoing_grads = (
        jnp.dot(placer, grad_blocks, preferred_element_type=jnp.float32)
        .astype(jnp.bfloat16)
        .reshape(EXPERTS, CAP, block_width)
    )

    def run_expert(expert_items):
        inputs, grads_in, w_in, w_out = expert_items
        outputs, grad_in, grad_out = expert_pass(
            inputs.reshape(-1, channels), grads_in.reshape(-1, channels), w_in, w_out
        )
        return (outputs.reshape(inputs.shape), grad_in, grad_out)

    arrived, arrived_grads = (
        lax.all_to_all(outgoing, "exp", split_axis=0, concat_axis=1, tiled=True),
        lax.all_to_all(outgoing_grads, "exp", split_axis=0, concat_axis=1, tiled=True),
    )
    results, grad_in, grad_out = lax.map(run_expert, (arrived, arrived_grads, exp_in, exp_out))
    returned = lax.all_to_all(results, "exp", split_axis=1, concat_axis=0, tiled=True)
    grad_in, grad_out = lax.psum((grad_in, grad_out), ("lat", "dp"))
    expert_out = jnp.dot(
        placer.T, returned.reshape(EXPERTS * CAP, block_width), preferred_element_type=jnp.float32
    ).astype(jnp.bfloat16)
    output = (
        dense_out.astype(jnp.float32) + expert_out.reshape(dense_out.shape).astype(jnp.float32)
    ).astype(jnp.bfloat16)
    return (output, grad_in, grad_out)


def solution(mesh):
    in_specs = (
        P(("dp", "exp"), "lat", None, None),
        P(("dp", "exp"), "lat", None, None),
        P(("dp", "exp"), "lat", None, None),
        P(),
        P(),
        P(),
        P(),
        P("exp", None, None),
        P("exp", None, None),
    )
    out_specs = (P(("dp", "exp"), "lat", None, None), P("exp", None, None), P("exp", None, None))
    return jax.shard_map(body, mesh=mesh, in_specs=in_specs, out_specs=out_specs, check_vma=False)
```

profile of v0, /device:TPU:2, one launch (start us, length us, event | category | flops | bytes accessed | tf_op | source)
XLA Modules:
  0.0 1631.7 jit_solution(9651882044922824037)
XLA Ops:
  9.0 4.0 collective-permute-start
  26.1 6.8 all-to-all-start.1
  38.0 26.9 %fusion.104 = (f32[16,256]{1,0:T(8,128)S(1)}, f32[1,16,256,192]{2,3,1,0:T(8,128)S(1)}) fusion(f32[192]{0:T(256)S(1)} %bitcast.170, bf16[1,22,262,192]{2,3,1,0:T(8,128)(2,1)S(1)} %fusion.69, f32[192]{0:T(256)S(1)} %bitcast.171, f32[192]{0:T(256)S(1)} %bitcast.143, f32[192]{0:T(256)S(1)} %bitcast.144, ...), kind=kLoop, calls=%fused_computation.138 | loop fusion | flops 115601408 | bytes 80270080 | tf_op jit(solution)/shard_map/reduce_sum | solution.py:48
  68.0 42.4 %fusion.60 = bf16[4096,192]{0,1:T(8,128)(2,1)} fusion(f32[4096,192]{0,1:T(8,128)S(1)} %bitcast.140, bf16[768,192]{0,1:T(8,128)(2,1)S(1)} %copy-done, bf16[4096,192]{0,1:T(8,128)(2,1)} %bitcast.141, bf16[192,768]{1,0:T(8,128)(2,1)} %param.16), kind=kOutput, calls=%fused_computation.83 | convolution fusion | flops 2621964288 | bytes 6881280 | tf_op jit(solution)/shard_map/dot_general | solution.py:55
  121.4 4.0 all-to-all-start
  131.9 27.7 %all-to-all-done = bf16[16,3,24576]{2,1,0:T(4,128)(2,1)S(1)} async-done(((bf16[16,3,24576]{2,1,0:T(4,128)(2,1)}), bf16[16,3,24576]{2,1,0:T(4,128)(2,1)S(1)}, u32[]{:S(2)}, u32[]{:S(2)}) %all-to-all-start) | async-done | bytes 2359328 | tf_op jit(solution)/shard_map/all_to_all | solution.py:107
  164.5 147.7 %while.14 = (s32[]{:T(128)}, bf16[8,6,24576]{2,1,0:T(8,128)(2,1)}, f32[8,192,768]{2,1,0:T(8,128)}, f32[8,768,192]{1,2,0:T(8,128)}, bf16[8,6,24576]{2,1,0:T(8,128...) while((s32[]{:T(128)}, bf16[8,6,24576]{2,1,0:T(8,128)(2,1)}, ...), condition=%wide.region_5.6_spmd, body=%wide.region_4.5_spmd.sunk | while | flops 1176846336 | bytes 16123001 | solution.py:110
  166.4 7.3 fusion.141
  184.8 7.3 fusion.141
  196.5 3.9 fusion.142
  203.2 7.3 fusion.141
  221.6 7.3 fusion.141
  233.4 3.9 fusion.142
  240.0 7.3 fusion.141
  251.8 3.9 fusion.142
  258.4 7.3 fusion.141
  276.8 7.3 fusion.141
  288.6 3.9 fusion.142
  295.2 7.3 fusion.141
  316.8 6.8 all-to-all-start.2
  326.6 22.0 %all-to-all-done.2 = bf16[8,6,24576]{2,0,1:T(8,128)(2,1)} async-done(((bf16[8,6,24576]{2,0,1:T(8,128)(2,1)}), bf16[8,6,24576]{2,0,1:T(8,128)(2,1)}, u32[]{:S(2)}, u32[]{:S(2)}) %all-to-all-start.2) | async-done | bytes 2359328 | tf_op jit(solution)/shard_map/all_to_all | solution.py:111
  360.9 4.0 add_convert_fusion
  367.2 1250.3 %all-reduce.4.cloned.1.call-done = (f32[8,192,768]{2,1,0:T(8,128)}, f32[8,768,192]{1,2,0:T(8,128)}) async-done(((f32[8,192,768]{2,1,0:T(8,128)}, f32[8,768,192]{1,2,0:T(8,128)}), (f32[8,192,768]{2,1,0:T(8,128)}, f32[8,768,192]{1,2,0:T(8,128)})) %all-reduce.4.cloned.1.call-update) | async-done | bytes 9437200 | tf_op jit(solution)/shard_map/psum | solution.py:112
  1617.5 5.0 copy.60
  (138 shorter events, 142.7 us)
Async XLA Ops:
  7.2 60.3 %copy-start = (bf16[768,192]{0,1:T(8,128)(2,1)S(1)}, bf16[768,192]{0,1:T(8,128)(2,1)}, u32[]{:S(2)}) copy-start(bf16[768,192]{0,1:T(8,128)(2,1)} %param.17) | copy-start | bytes 884740
  9.0 24.0 %collective-permute-start = (bf16[1,3,256,192]{2,3,1,0:T(8,128)(2,1)}, bf16[1,3,256,192]{2,3,1,0:T(8,128)(2,1)S(1)}, u32[]{:S(2)}, u32[]{:S(2)}) collective-permute-start(bf16[1,3,256,192]{2,3,1,0:T(8,128)(2,1)} %get-tuple-element.88), channel_id=1, source_target_pairs={{0,128},{1,129},{2,130},{3,131},{4,132},{5,133},{6,134},{7,135},{8... | collective-permute-start | bytes 884744 | tf_op jit(solution)/shard_map/ppermute | solution.py:16
  13.1 22.7 %collective-permute-start.1 = (bf16[1,3,256,192]{2,3,1,0:T(8,128)(2,1)S(1)}, bf16[1,3,256,192]{2,3,1,0:T(8,128)(2,1)S(1)}, u32[]{:S(2)}, u32[]{:S(2)}) collective-permute-start(bf16[1,3,256,192]{2,3,1,0:T(8,128)(2,1)S(1)} %get-tuple-element.89), channel_id=1, source_target_pairs={{128,0},{129,1},{130,2},{131,3},{132,4},{133,5},{134,6},{135,7},{1... | collective-permute-start | bytes 884744 | tf_op jit(solution)/shard_map/ppermute | solution.py:19
  26.1 6.8 copy-start.6
  26.1 6.9 copy-start.2
  26.1 95.2 %all-to-all-start.1 = ((bf16[16,3,24576]{2,1,0:T(4,128)(2,1)}), bf16[16,3,24576]{2,1,0:T(4,128)(2,1)}, u32[]{:S(2)}, u32[]{:S(2)}) async-start(bf16[16,3,24576]{2,1,0:T(4,128)(2,1)} %reshape.262), calls=%async_computation.1 | async-start | bytes 6291456 | tf_op jit(solution)/shard_map/all_to_all | solution.py:108
  64.9 0.7 copy-start.7
  65.6 2.4 copy-start.4
  121.4 38.3 %all-to-all-start = ((bf16[16,3,24576]{2,1,0:T(4,128)(2,1)}), bf16[16,3,24576]{2,1,0:T(4,128)(2,1)S(1)}, u32[]{:S(2)}, u32[]{:S(2)}) async-start(bf16[16,3,24576]{2,1,0:T(4,128)(2,1)} %reshape.260), calls=%async_computation | async-start | bytes 6291456 | tf_op jit(solution)/shard_map/all_to_all | solution.py:107
  125.3 1492.2 %all-reduce.4.cloned.1.call-start = ((), (), s32[]{:S(2)}) async-start(), calls=%async_computation.3 | async-start | bytes 18874368 | tf_op jit(solution)/shard_map/psum | solution.py:112
  312.2 1.9 copy-start.5
  316.8 6.8 copy-start.3
  316.8 31.9 %all-to-all-start.2 = ((bf16[8,6,24576]{2,0,1:T(8,128)(2,1)}), bf16[8,6,24576]{2,0,1:T(8,128)(2,1)}, u32[]{:S(2)}, u32[]{:S(2)}) async-start(bf16[8,6,24576]{2,0,1:T(8,128)(2,1)} %copy.28), calls=%async_computation.2 | async-start | bytes 4718592 | tf_op jit(solution)/shard_map/all_to_all | solution.py:111
  1617.5 5.0 slice-start
  1617.5 5.0 slice-start.1
  1617.5 7.2 copy-start.1
Sparse Core Ops, SparseCore 0:
  312.3 1305.1 all-reduce.3
where the time goes:
time: 1640 us; the launch traced here: 1630 us
  waiting for transfers between devices  1300 us (79%)
  matrix products  161 us (10%)
  local copies, waits for them, and re-layouts  98.1 us (6%)
  other arithmetic  35 us (2%)
  starting transfers between devices  22.9 us (1%)
    psum x1, waiting for transfers between devices, body(): grad_in, grad_out = lax.psum((grad_in, grad_out), ('lat', 'dp'))  1250 us
    dot_general x8, matrix products, expert_pass(): pre_act = jnp.dot(inputs, w_in, preferred_element_type=jnp.float32)  58.5 us
    dot_general x1, matrix products, dense_block(): reduced = jnp.dot(active, w_reduce, preferred_element_type=jnp.float32)  42.4 us
  transfers between devices with their start and end apart: 6, of which 3 were waited for; matrix products, arithmetic and copies ran while one was open for 8% of the time, Pallas kernels for 0%

commit v1 on v0

--- a/solution.py
+++ b/solution.py
@@ -109,7 +109,8 @@
     )
     results, grad_in, grad_out = lax.map(run_expert, (arrived, arrived_grads, exp_in, exp_out))
     returned = lax.all_to_all(results, "exp", split_axis=1, concat_axis=0, tiled=True)
-    grad_in, grad_out = lax.psum((grad_in, grad_out), ("lat", "dp"))
+    do_slices = lambda local, which_axis, a_name: lax.psum(lax.psum(local, which_axis), a_name)
+    grad_in, grad_out = do_slices((grad_in, grad_out), "dp", "lat")
     expert_out = jnp.dot(
         placer.T, returned.reshape(EXPERTS * CAP, block_width), preferred_element_type=jnp.float32
     ).astype(jnp.bfloat16)

time: 1640 us -> 802 us (0.49)
  waiting for transfers between devices: 1300 us -> 460 us
    psum x1 -> x2, waiting for transfers between devices: 1250 us -> 389 us  [the longest x1 213 us: body(): lax.psum(local, which_axis)]
    all_to_all x1, waiting for transfers between devices: 22 us -> 42.6 us  [body(): lax.all_to_all(results, 'exp', split_axis=1, concat_axis=0, tiled=True)]
  transfers between devices with their start and end apart: 6 -> 7, of which waited for: 3 -> 4; matrix products, arithmetic and copies ran while one was open for 8% -> 17% of each run, Pallas kernels for 0% -> 0%
where the time goes in v1:
time: 802 us; the launch traced here: 792 us
  waiting for transfers between devices  460 us (57%)
  matrix products  161 us (20%)
  local copies, waits for them, and re-layouts  101 us (13%)
  other arithmetic  35.4 us (4%)
  starting transfers between devices  20.5 us (3%)
  between operations  14.5 us (2%)
    psum x1, waiting for transfers between devices, body(): lax.psum(local, which_axis)  213 us
    psum x1, waiting for transfers between devices, body(): lax.psum(lax.psum(local, which_axis), a_name)  177 us
    dot_general x8, matrix products, expert_pass(): pre_act = jnp.dot(inputs, w_in, preferred_element_type=jnp.float32)  58.7 us
    all_to_all x1, waiting for transfers between devices, body(): lax.all_to_all(results, 'exp', split_axis=1, concat_axis=0, tiled=True)  42.6 us
    dot_general x1, matrix products, dense_block(): reduced = jnp.dot(active, w_reduce, preferred_element_type=jnp.float32)  42.4 us
    dot_general x8, matrix products, expert_pass(): grad_in = jnp.dot(inputs.T, scaled, preferred_element_type=jnp.float32)  31 us
    all_to_all x1, waiting for transfers between devices, body(): lax.all_to_all(outgoing, 'exp', split_axis=0, concat_axis=1, tiled=True)  27.7 us
    reduce_sum x1, other arithmetic, dense_block(): channel_mean = jnp.mean(smoothed, axis=-1, keepdims=True)  26.9 us
  transfers between devices with their start and end apart: 7, of which 4 were waited for; matrix products, arithmetic and copies ran while one was open for 17% of the time, Pallas kernels for 0%

profile of v1, /device:TPU:2, one launch (start us, length us, event | category | flops | bytes accessed | tf_op | source)
XLA Modules:
  0.0 791.9 jit_solution(1799531077816769084)
XLA Ops:
  9.0 4.0 collective-permute-start
  26.1 6.8 all-to-all-start.1
  38.0 26.9 %fusion.104 = (f32[16,256]{1,0:T(8,128)S(1)}, f32[1,16,256,192]{2,3,1,0:T(8,128)S(1)}) fusion(f32[192]{0:T(256)S(1)} %bitcast.171, bf16[1,22,262,192]{2,3,1,0:T(8,128)(2,1)S(1)} %fusion.69, f32[192]{0:T(256)S(1)} %bitcast.172, f32[192]{0:T(256)S(1)} %bitcast.144, f32[192]{0:T(256)S(1)} %bitcast.145, ...), kind=kLoop, calls=%fused_computation.138 | loop fusion | flops 115601408 | bytes 80270080 | tf_op jit(solution)/shard_map/reduce_sum | solution.py:48
  68.0 42.4 %fusion.60 = bf16[4096,192]{0,1:T(8,128)(2,1)} fusion(f32[4096,192]{0,1:T(8,128)S(1)} %bitcast.141, bf16[768,192]{0,1:T(8,128)(2,1)S(1)} %copy-done, bf16[4096,192]{0,1:T(8,128)(2,1)} %bitcast.142, bf16[192,768]{1,0:T(8,128)(2,1)} %param.16), kind=kOutput, calls=%fused_computation.83 | convolution fusion | flops 2621964288 | bytes 6881280 | tf_op jit(solution)/shard_map/dot_general | solution.py:55
  121.4 4.0 all-to-all-start
  132.0 27.7 %all-to-all-done = bf16[16,3,24576]{2,1,0:T(4,128)(2,1)S(1)} async-done(((bf16[16,3,24576]{2,1,0:T(4,128)(2,1)}), bf16[16,3,24576]{2,1,0:T(4,128)(2,1)S(1)}, u32[]{:S(2)}, u32[]{:S(2)}) %all-to-all-start) | async-done | bytes 2359328 | tf_op jit(solution)/shard_map/all_to_all | solution.py:107
  164.4 147.8 %while.14 = (s32[]{:T(128)}, bf16[8,6,24576]{2,1,0:T(8,128)(2,1)}, f32[8,192,768]{2,1,0:T(8,128)}, f32[8,768,192]{1,2,0:T(8,128)}, bf16[8,6,24576]{2,1,0:T(8,128...) while((s32[]{:T(128)}, bf16[8,6,24576]{2,1,0:T(8,128)(2,1)}, ...), condition=%wide.region_5.6_spmd, body=%wide.region_4.5_spmd.sunk | while | flops 1176846336 | bytes 16123001 | solution.py:110
  166.3 7.3 fusion.141
  184.8 7.3 fusion.141
  196.6 3.9 fusion.142
  203.2 7.3 fusion.141
  221.6 7.3 fusion.141
  240.0 7.3 fusion.141
  251.8 3.9 fusion.142
  258.4 7.3 fusion.141
  276.9 7.3 fusion.141
  295.3 7.3 fusion.141
  312.3 212.8 %all-reduce.6.cloned.1.call-done = (f32[8,192,768]{2,1,0:T(8,128)}, f32[8,768,192]{1,2,0:T(8,128)}) async-done(((f32[8,192,768]{2,1,0:T(8,128)}, f32[8,768,192]{1,2,0:T(8,128)}), (f32[8,192,768]{2,1,0:T(8,128)}, f32[8,768,192]{1,2,0:T(8,128)})) %all-reduce.6.cloned.1.call-update) | async-done | bytes 9437200 | tf_op jit(solution)/shard_map/psum | solution.py:112
  529.7 4.4 all-to-all-start.2
  534.0 4.2 copy.32
  538.2 42.6 %all-to-all-done.2 = bf16[8,6,24576]{2,0,1:T(8,128)(2,1)S(1)} async-done(((bf16[8,6,24576]{2,0,1:T(8,128)(2,1)}), bf16[8,6,24576]{2,0,1:T(8,128)(2,1)S(1)}, u32[]{:S(2)}, u32[]{:S(2)}) %all-to-all-start.2) | async-done | bytes 2359328 | tf_op jit(solution)/shard_map/all_to_all | solution.py:111
  594.4 4.4 add_convert_fusion
  601.1 176.6 %all-reduce.8.cloned.1.call-done = (f32[8,192,768]{2,1,0:T(8,128)}, f32[8,768,192]{1,2,0:T(8,128)}) async-done(((f32[8,192,768]{2,1,0:T(8,128)}, f32[8,768,192]{1,2,0:T(8,128)}), (f32[8,192,768]{2,1,0:T(8,128)}, f32[8,768,192]{1,2,0:T(8,128)})) %all-reduce.8.cloned.1.call-update) | async-done | bytes 9437200 | tf_op jit(solution)/shard_map/psum | solution.py:112
  777.7 5.0 copy.62
  (141 shorter events, 148.8 us)
Async XLA Ops:
  7.2 60.3 %copy-start = (bf16[768,192]{0,1:T(8,128)(2,1)S(1)}, bf16[768,192]{0,1:T(8,128)(2,1)}, u32[]{:S(2)}) copy-start(bf16[768,192]{0,1:T(8,128)(2,1)} %param.17) | copy-start | bytes 884740
  9.0 23.9 %collective-permute-start = (bf16[1,3,256,192]{2,3,1,0:T(8,128)(2,1)}, bf16[1,3,256,192]{2,3,1,0:T(8,128)(2,1)S(1)}, u32[]{:S(2)}, u32[]{:S(2)}) collective-permute-start(bf16[1,3,256,192]{2,3,1,0:T(8,128)(2,1)} %get-tuple-element.90), channel_id=1, source_target_pairs={{0,128},{1,129},{2,130},{3,131},{4,132},{5,133},{6,134},{7,135},{8... | collective-permute-start | bytes 884744 | tf_op jit(solution)/shard_map/ppermute | solution.py:16
  13.1 22.6 %collective-permute-start.1 = (bf16[1,3,256,192]{2,3,1,0:T(8,128)(2,1)S(1)}, bf16[1,3,256,192]{2,3,1,0:T(8,128)(2,1)S(1)}, u32[]{:S(2)}, u32[]{:S(2)}) collective-permute-start(bf16[1,3,256,192]{2,3,1,0:T(8,128)(2,1)S(1)} %get-tuple-element.91), channel_id=1, source_target_pairs={{128,0},{129,1},{130,2},{131,3},{132,4},{133,5},{134,6},{135,7},{1... | collective-permute-start | bytes 884744 | tf_op jit(solution)/shard_map/ppermute | solution.py:19
  26.1 6.8 copy-start.6
  26.1 6.9 copy-start.2
  26.1 95.3 %all-to-all-start.1 = ((bf16[16,3,24576]{2,1,0:T(4,128)(2,1)}), bf16[16,3,24576]{2,1,0:T(4,128)(2,1)}, u32[]{:S(2)}, u32[]{:S(2)}) async-start(bf16[16,3,24576]{2,1,0:T(4,128)(2,1)} %reshape.262), calls=%async_computation.1 | async-start | bytes 6291456 | tf_op jit(solution)/shard_map/all_to_all | solution.py:108
  64.9 0.7 copy-start.7
  65.6 2.4 copy-start.4
  121.4 38.3 %all-to-all-start = ((bf16[16,3,24576]{2,1,0:T(4,128)(2,1)}), bf16[16,3,24576]{2,1,0:T(4,128)(2,1)S(1)}, u32[]{:S(2)}, u32[]{:S(2)}) async-start(bf16[16,3,24576]{2,1,0:T(4,128)(2,1)} %reshape.260), calls=%async_computation | async-start | bytes 6291456 | tf_op jit(solution)/shard_map/all_to_all | solution.py:107
  125.4 399.7 %all-reduce.6.cloned.1.call-start = ((), (), s32[]{:S(2)}) async-start(), calls=%async_computation.3 | async-start | bytes 18874368 | tf_op jit(solution)/shard_map/psum | solution.py:112
  312.2 465.5 %all-reduce.8.cloned.1.call-start = ((), (), s32[]{:S(2)}) async-start(), calls=%async_computation.4 | async-start | bytes 18874368 | tf_op jit(solution)/shard_map/psum | solution.py:112
  525.1 1.9 copy-start.5
  529.7 51.2 %all-to-all-start.2 = ((bf16[8,6,24576]{2,0,1:T(8,128)(2,1)}), bf16[8,6,24576]{2,0,1:T(8,128)(2,1)S(1)}, u32[]{:S(2)}, u32[]{:S(2)}) async-start(bf16[8,6,24576]{2,0,1:T(8,128)(2,1)} %copy.28), calls=%async_computation.2 | async-start | bytes 4718592 | tf_op jit(solution)/shard_map/all_to_all | solution.py:111
  580.8 1.4 copy-start.3
  777.7 5.0 slice-start
  777.7 5.0 slice-start.1
  777.7 7.2 copy-start.1
Sparse Core Ops, SparseCore 0:
  312.4 212.6 all-reduce.5
  528.1 249.5 all-reduce.7
